TPU v7x, 256 devices: a whole 4x4x8 slice. The times are simulated.
256 devices in a mesh: row: 64 (over x, z, core), col: 4 (over y).
Axes of the slice: x: 4, y: 4, z: 8, core: 2. Of those that a mesh axis runs over, the one named last changes fastest.
Arguments:
- matrix: float32 [128, 4194304], P('col', 'row'), may hold values from -200 to 200
- row_signs: int32 [4194304], P('row'), may hold values from -1 to 1, as said below
- sample_rows: int32 [2048], replicated, may hold values from 0 to 4194303, as said below
- target: float32 [4194304], P('row'), may hold values from -6 to 6
Outputs:
- gradient: float32 [128], replicated
- residual: float32 [4194304], P('row')
Inputs may be any that keep to these rules, and one draw needn't show every extreme that they name: `row_signs`: each entry is -1 or +1. `sample_rows`: indices may repeat; 0 and 4194303 are always among them.
All inputs are finite; a program needn't handle non-finite values.
Results may differ from a plain program's by a relative error of at most 0.0003.
Values sent between devices are 32-bit elements; how exact they have to be, the bound alone decides.
No kernel may reach another device: no remote copies, remote signals or barrier semaphores. Data moves between devices by JAX's collectives and lax.ppermute only.
A program may use at most 128 MiB of HBM per device.

v0:
```python
import jax
import jax.numpy as jnp
from jax import lax
from jax.sharding import PartitionSpec as P


def walsh_transform(order):
    index = jnp.arange(order, dtype=jnp.int32)
    common = jnp.bitwise_and(index[:, None], index[None, :])
    parity = jnp.zeros((order, order), jnp.int32)
    for shift in range(max(order.bit_length() - 1, 1)):
        parity = parity + jnp.bitwise_and(jnp.right_shift(common, shift), 1)
    return (1 - 2 * (parity % 2)).astype(jnp.float32)


def body(matrix, row_signs, sample_rows, target):
    upper_limit = lax.Precision.HIGHEST
    cols_dev, rows_dev = matrix.shape
    row_count = lax.axis_size("row")
    my_index = lax.axis_index("row")
    total_rows = rows_dev * row_count
    slice_len = rows_dev // row_count
    inv_root = 1.0 / jnp.sqrt(jnp.float32(total_rows))
    signed = matrix * row_signs.astype(jnp.float32)[None, :]
    block_list = signed.reshape(cols_dev, rows_dev // 128, 128)
    block_list = jnp.einsum("cbt,ts->cbs", block_list, walsh_transform(128), precision=upper_limit)
    block_list = jnp.einsum(
        "cbs,ba->cas", block_list, walsh_transform(rows_dev // 128), precision=upper_limit
    )
    spread = block_list.reshape(cols_dev, row_count, slice_len)
    arrived = lax.all_to_all(spread, "row", split_axis=1, concat_axis=1, tiled=True)
    mixed = jnp.einsum("cpj,pk->ckj", arrived, walsh_transform(row_count), precision=upper_limit)
    mixed = mixed * inv_root
    local_rows = lax.all_to_all(mixed, "row", split_axis=1, concat_axis=1, tiled=True).reshape(
        cols_dev, rows_dev
    )
    owner_dev = sample_rows // rows_dev
    where_at = sample_rows % rows_dev
    chosen = jnp.where(
        (owner_dev == my_index)[None, :], jnp.take(local_rows, where_at, axis=1), 0.0
    )
    rhs_part = jnp.dot(matrix, target, precision=upper_limit)
    weight = total_rows / sample_rows.shape[0]
    selected_row_sum, rhs_sum = lax.psum((chosen, rhs_part), "row")
    whole_cols, rhs_all = (
        lax.all_gather(selected_row_sum, "col", axis=0, tiled=True),
        lax.all_gather(rhs_sum, "col", axis=0, tiled=True),
    )
    cross_product_matrix = jnp.dot(whole_cols, whole_cols.T, precision=upper_limit) * weight
    lower = jnp.linalg.cholesky(cross_product_matrix)
    gradient = lax.linalg.triangular_solve(lower, rhs_all[:, None], left_side=True, lower=True)[
        :, 0
    ]
    estimate = lax.linalg.triangular_solve(
        lower, gradient[:, None], left_side=True, lower=True, transpose_a=True
    )[:, 0]
    col_index = lax.axis_index("col")
    local_estimate = lax.dynamic_slice_in_dim(estimate, col_index * cols_dev, cols_dev, 0)
    fitted_portion = jnp.dot(local_estimate, matrix, precision=upper_limit)
    fitted = lax.psum(fitted_portion, "col")
    return (gradient, target - fitted)


def solution(mesh):
    return jax.shard_map(
        body,
        mesh=mesh,
        in_specs=(P("col", "row"), P("row"), P(), P("row")),
        out_specs=(P(), P("row")),
        check_vma=False,
    )
```

profile of v0, /device:TPU:2, one launch (start us, length us, event | category | flops | bytes accessed | tf_op | source)
XLA Modules:
  0.0 919.7 jit_solution(17685823326387873341)
XLA Ops:
  7.2 1.0 convert_element_type.14
  8.1 4.1 multiply_bitcast_fusion.1
  12.3 1.5 copy.14
  13.7 8.6 fusion.28
  22.3 18.4 %convolution_bitcast_fusion = f32[32,512,128]{2,1,0:T(8,128)} fusion(f32[32,512,128]{2,1,0:T(8,128)S(1)} %fusion.28), kind=kOutput, calls=%fused_computation.5 | convolution fusion | flops 12895649792 | bytes 16777216 | tf_op jit(solution)/shard_map/cbs,ba->cas/dot_general | solution.py:27
  40.7 9.4 %reshape.41 = f32[32,64,1024]{2,1,0:T(8,128)} reshape(f32[32,512,128]{2,1,0:T(8,128)} %convolution_bitcast_fusion) | data formatting | bytes 16777216 | tf_op jit(solution)/shard_map/reshape | solution.py:30
  50.1 8.2 copy.8
  58.4 196.0 %all_to_all.10 = f32[32,64,1024]{2,0,1:T(8,128)S(1)} all-to-all(f32[32,64,1024]{2,0,1:T(8,128)S(1)} %copy.8), channel_id=1, replica_groups=mesh['row'=64,'col'=4] {'row'}, dimensions={1} | all-to-all | bytes 16777216 | tf_op jit(solution)/shard_map/all_to_all | solution.py:31
  254.3 12.5 %multiply_bitcast_fusion = f32[32,64,1024]{2,1,0:T(8,128)S(1)} fusion(f32[32,64,1024]{2,0,1:T(8,128)S(1)} %all_to_all.10), kind=kOutput, calls=%fused_computation.3 | convolution fusion | flops 1612840960 | bytes 16777216 | tf_op jit(solution)/shard_map/cpj,pk->ckj/dot_general | solution.py:32
  266.8 8.5 copy.10
  275.3 0.0 copy-start.1
  275.3 8.1 all-to-all-start.1
  283.3 0.0 all-reduce.4.cloned.1.call-start
  283.4 0.0 copy-done.1
  283.5 0.0 copy-start.3
  283.5 0.0 copy-start
  283.5 184.1 %all-to-all-done.1 = f32[32,64,1024]{2,0,1:T(8,128)} async-done(((f32[32,64,1024]{2,0,1:T(8,128)}), f32[32,64,1024]{2,0,1:T(8,128)}, u32[]{:S(2)}, u32[]{:S(2)}) %all-to-all-start.1) | async-done | bytes 8388640 | tf_op jit(solution)/shard_map/all_to_all | solution.py:34
  467.6 19.6 %copy.11 = f32[32,64,1024]{0,2,1:T(8,128)} copy(f32[32,64,1024]{2,0,1:T(8,128)} %all-to-all-done.1) | data formatting | bytes 16777216 | tf_op jit(solution)/shard_map/all_to_all | solution.py:34
  487.2 16.0 %gather_fusion = f32[2048,32]{1,0:T(8,128)S(1)} fusion(f32[32,65536]{0,1:T(8,128)} %bitcast.55, s32[2048]{0:T(1024)S(1)} %broadcast_clamp_fusion), kind=kCustom, calls=%fused_computation | custom fusion | bytes 532480 | tf_op jit(solution)/shard_map/jit(_take)/gather | solution.py:40
  503.2 2.4 select_bitcast_fusion
  505.6 0.0 all-reduce.4.cloned.1.call-update
  505.7 0.0 all-gather.2.cloned.1.call-start
  505.7 185.2 %all-reduce.4.cloned.1.call-done = f32[32,2048]{0,1:T(8,128)} async-done(((f32[32,2048]{0,1:T(8,128)}), f32[32,2048]{0,1:T(8,128)}) %all-reduce.4.cloned.1.call-update) | async-done | bytes 262160 | tf_op jit(solution)/shard_map/psum | solution.py:44
  690.9 2.2 copy.12
  693.2 0.0 all-gather.2.cloned.1.call-update
  693.2 0.0 all-reduce.6.cloned.1.call-start
  693.3 0.0 copy-done.3
  693.3 0.6 dynamic-slice.1
  694.5 0.0 copy-done
  694.5 8.9 convolution_bitcast_fusion.1
  703.4 104.7 %psum.22 = f32[32]{0:T(128)S(1)} all-reduce(f32[32]{0:T(128)S(1)} %convolution_bitcast_fusion.1), channel_id=1, replica_groups=mesh['row'=64,'col'=4] {'row'}, use_global_device_ids=true, to_apply=%region_3.4 | all-reduce | flops 32 | bytes 256 | tf_op jit(solution)/shard_map/psum | solution.py:44
  808.1 0.2 dynamic-update-slice.3
  808.3 10.7 %all-reduce = f32[128]{0:T(128)S(1)} all-reduce(f32[128]{0:T(128)S(1)} %dynamic-update-slice.3), channel_id=1, replica_groups=mesh['row'=64,'col'=4] {'col'}, use_global_device_ids=true, to_apply=%add | all-reduce | flops 128 | bytes 1024
  819.0 0.0 all-gather.2.cloned.1.call-done
  819.1 2.5 fusion.89
  821.6 0.1 copy.13
  821.7 11.7 %cholesky.16 = f32[128,128]{1,0:T(8,128)S(1)} custom-call(f32[128,128]{1,0:T(8,128)S(1)} %fusion.33), custom_call_target="Cholesky" | custom-call | tf_op jit(solution)/shard_map/jit(cholesky)/cholesky | solution.py:50
  833.5 0.6 compare_reduce_fusion
  834.1 0.7 fusion.22
  834.8 9.8 %custom-call.8 = f32[1,128,128]{1,2,0:T(8,128)S(1)} custom-call(f32[1,128,128]{2,1,0:T(8,128)S(1)} %fusion.22), custom_call_target="InvertDiagBlocksLowerTriangular" | custom-call | tf_op jit(solution)/shard_map/triangular_solve | solution.py:51
  844.6 0.2 fusion.31
  844.7 0.0 copy-start.2
  844.7 0.2 convolution_bitcast_fusion.2
  844.9 7.1 fusion.62
  852.0 0.0 all-reduce.6.cloned.1.call-update
  852.0 59.2 %all-reduce.6.cloned.1.call-done = f32[65536]{0:T(1024)} async-done(((f32[65536]{0:T(1024)}), f32[65536]{0:T(1024)}) %all-reduce.6.cloned.1.call-update) | async-done | bytes 262160 | tf_op jit(solution)/shard_map/psum | solution.py:60
  911.3 1.7 sub.22
  912.9 0.0 copy-done.2
  (5 shorter events, 0.1 us)
Async XLA Ops:
  275.3 8.1 copy-start.1
  275.3 192.3 %all-to-all-start.1 = ((f32[32,64,1024]{2,0,1:T(8,128)}), f32[32,64,1024]{2,0,1:T(8,128)}, u32[]{:S(2)}, u32[]{:S(2)}) async-start(f32[32,64,1024]{2,0,1:T(8,128)} %copy.10), calls=%async_computation.1 | async-start | bytes 16777216 | tf_op jit(solution)/shard_map/all_to_all | solution.py:34
  283.3 407.6 %all-reduce.4.cloned.1.call-start = ((), (), s32[]{:S(2)}) async-start(), calls=%async_computation.2 | async-start | bytes 2097152 | tf_op jit(solution)/shard_map/psum | solution.py:44
  283.5 409.8 %copy-start.3 = (u32[256]{0:T(256)S(1)}, u32[256]{0:T(256)}, u32[]{:S(2)}) copy-start(u32[256]{0:T(256)} %constant.164) | copy-start | bytes 3076
  283.5 411.0 %copy-start = (f32[65536]{0:T(1024)S(1)}, f32[65536]{0:T(1024)}, u32[]{:S(2)}) copy-start(f32[65536]{0:T(1024)} %param.7) | copy-start | bytes 786436
  505.7 313.4 %all-gather.2.cloned.1.call-start = ((), (), s32[]{:S(2)}) async-start(), calls=%async_computation.3 | async-start | bytes 1310720 | tf_op jit(solution)/shard_map/all_gather | solution.py:46
  693.2 218.1 %all-reduce.6.cloned.1.call-start = ((), (), s32[]{:S(2)}) async-start(), calls=%async_computation.4 | async-start | bytes 524288 | tf_op jit(solution)/shard_map/psum | solution.py:60
  844.7 68.2 %copy-start.2 = (f32[1,128]{1,0:T(1,128)}, f32[1,128]{1,0:T(1,128)S(1)}, u32[]{:S(2)}) copy-start(f32[1,128]{1,0:T(1,128)S(1)} %fusion.31) | copy-start | bytes 1540
Sparse Core Ops, SparseCore 0:
  505.8 185.1 all-reduce.3
  693.3 23.8 all-gather.1
  852.1 59.0 all-reduce.5
where the time goes:
time: 923 us; the launch traced here: 920 us
  waiting for transfers between devices  429 us (46%)
  blocking collectives  311 us (34%)
  local copies, waits for them, and re-layouts  66.4 us (7%)
  matrix products  58.3 us (6%)
  other arithmetic  32.1 us (3%)
  between operations  14.8 us (2%)
    all_to_all x1, blocking collectives, body(): lax.all_to_all(spread, 'row', split_axis=1, concat_axis=1, tiled=True)  196 us
    psum x1, waiting for transfers between devices, body(): selected_row_sum, rhs_sum = lax.psum((chosen, rhs_part), 'row')  185 us
    all_to_all x1, waiting for transfers between devices, body(): lax.all_to_all(mixed, 'row', split_axis=1, concat_axis=1, tiled=True)  184 us
    psum x1, blocking collectives, body(): selected_row_sum, rhs_sum = lax.psum((chosen, rhs_part), 'row')  105 us
    psum x1, waiting for transfers between devices, body(): fitted = lax.psum(fitted_portion, 'col')  59.2 us
    all_to_all x1, local copies, waits for them, and re-layouts, body(): lax.all_to_all(mixed, 'row', split_axis=1, concat_axis=1, tiled=True)  19.6 us
  transfers between devices with their start and end apart: 4, of which 3 were waited for; matrix products, arithmetic and copies ran while one was open for 1% of the time, Pallas kernels for 0%

commit v1 on v0

--- a/solution.py
+++ b/solution.py
@@ -2,6 +2,13 @@
 import jax.numpy as jnp
 from jax import lax
 from jax.sharding import PartitionSpec as P
+
+_manage_screen = lambda u: jnp.concatenate(
+    lax.all_to_all(
+        jnp.stack(jnp.split(u, lax.axis_size("row"), axis=1)), "row", split_axis=0, concat_axis=0
+    ),
+    1,
+)
 
 
 def walsh_transform(order):
@@ -28,7 +35,7 @@
         "cbs,ba->cas", block_list, walsh_transform(rows_dev // 128), precision=upper_limit
     )
     spread = block_list.reshape(cols_dev, row_count, slice_len)
-    arrived = lax.all_to_all(spread, "row", split_axis=1, concat_axis=1, tiled=True)
+    arrived = _manage_screen(spread)
     mixed = jnp.einsum("cpj,pk->ckj", arrived, walsh_transform(row_count), precision=upper_limit)
     mixed = mixed * inv_root
     local_rows = lax.all_to_all(mixed, "row", split_axis=1, concat_axis=1, tiled=True).reshape(

time: 923 us -> 950 us (1.029)
  local copies, waits for them, and re-layouts: 66.4 us -> 92.8 us
    split x0 -> x4, local copies, waits for them, and re-layouts: none -> 33 us  [jnp.split(u, lax.axis_size('row'), axis=1)]
where the time goes in v1:
time: 950 us; the launch traced here: 947 us
  waiting for transfers between devices  429 us (45%)
  blocking collectives  311 us (33%)
  local copies, waits for them, and re-layouts  92.8 us (10%)
  matrix products  58.3 us (6%)
  other arithmetic  32.1 us (3%)
  between operations  15.3 us (2%)
    all_to_all x1, blocking collectives, lax.all_to_all(jnp.stack(jnp.split(u, lax.axis_size('row'), axis=1)), 'ro...  196 us
    psum x1, waiting for transfers between devices, body(): selected_row_sum, rhs_sum = lax.psum((chosen, rhs_part), 'row')  185 us
    all_to_all x1, waiting for transfers between devices, body(): lax.all_to_all(mixed, 'row', split_axis=1, concat_axis=1, tiled=True)  184 us
    psum x1, blocking collectives, body(): selected_row_sum, rhs_sum = lax.psum((chosen, rhs_part), 'row')  105 us
    psum x1, waiting for transfers between devices, body(): fitted = lax.psum(fitted_portion, 'col')  59.2 us
    split x4, local copies, waits for them, and re-layouts, jnp.split(u, lax.axis_size('row'), axis=1)  33 us
    all_to_all x1, local copies, waits for them, and re-layouts, body(): lax.all_to_all(mixed, 'row', split_axis=1, concat_axis=1, tiled=True)  19.5 us
  transfers between devices with their start and end apart: 4, of which 3 were waited for; matrix products, arithmetic and copies ran while one was open for 1% of the time, Pallas kernels for 0%

profile of v1, /device:TPU:2, one launch (start us, length us, event | category | flops | bytes accessed | tf_op | source)
XLA Modules:
  0.0 946.7 jit_solution(11927991178455147520)
XLA Ops:
  7.2 1.0 convert_element_type.14
  8.1 4.1 multiply_bitcast_fusion.1
  12.3 1.5 copy.204
  13.7 8.6 fusion.29
  22.3 18.4 %convolution_bitcast_fusion = f32[32,512,128]{2,1,0:T(8,128)} fusion(f32[32,512,128]{2,1,0:T(8,128)S(1)} %fusion.29), kind=kOutput, calls=%fused_computation.6 | convolution fusion | flops 12895649792 | bytes 16777216 | tf_op jit(solution)/shard_map/cbs,ba->cas/dot_general | solution.py:34
  40.7 9.3 reshape.47
  50.0 5.4 fusion.93
  55.4 9.3 fusion.92
  64.7 9.0 fusion.91
  73.7 9.3 fusion.90
  85.3 196.0 %all_to_all.10 = f32[64,32,1,1024]{3,1,2,0:T(8,128)S(1)} all-to-all(f32[64,32,1,1024]{3,1,2,0:T(8,128)S(1)} %constant_dynamic-update-slice_fusion), channel_id=1, replica_groups=mesh['row'=64,'col'=4] {'row'}, dimensions={0} | all-to-all | bytes 16777216 | tf_op jit(solution)/shard_map/all_to_all | solution.py:7
  281.2 12.5 %multiply_bitcast_fusion = f32[32,64,1024]{2,1,0:T(8,128)S(1)} fusion(f32[64,32,1,1024]{3,1,2,0:T(8,128)S(1)} %all_to_all.10), kind=kOutput, calls=%fused_computation.4 | convolution fusion | flops 1612840960 | bytes 16777216 | tf_op jit(solution)/shard_map/cpj,pk->ckj/dot_general | solution.py:39
  293.7 8.5 copy.136
  302.2 8.0 all-to-all-start.1
  310.2 0.0 all-reduce.4.cloned.1.call-start
  310.3 0.0 copy-done.1
  310.4 0.0 copy-start.3
  310.4 0.0 copy-start
  310.4 184.1 %all-to-all-done.1 = f32[32,64,1024]{2,0,1:T(8,128)} async-done(((f32[32,64,1024]{2,0,1:T(8,128)}), f32[32,64,1024]{2,0,1:T(8,128)}, u32[]{:S(2)}, u32[]{:S(2)}) %all-to-all-start.1) | async-done | bytes 8388640 | tf_op jit(solution)/shard_map/all_to_all | solution.py:41
  494.5 19.5 %copy.137 = f32[32,64,1024]{0,2,1:T(8,128)} copy(f32[32,64,1024]{2,0,1:T(8,128)} %all-to-all-done.1) | data formatting | bytes 16777216 | tf_op jit(solution)/shard_map/all_to_all | solution.py:41
  514.0 16.0 %gather_fusion = f32[2048,32]{1,0:T(8,128)S(1)} fusion(f32[32,65536]{0,1:T(8,128)} %bitcast.318, s32[2048]{0:T(1024)S(1)} %broadcast_clamp_fusion), kind=kCustom, calls=%fused_computation | custom fusion | bytes 532480 | tf_op jit(solution)/shard_map/jit(_take)/gather | solution.py:47
  530.0 2.4 select_bitcast_fusion
  532.4 0.0 all-reduce.4.cloned.1.call-update
  532.5 0.0 all-gather.2.cloned.1.call-start
  532.5 185.4 %all-reduce.4.cloned.1.call-done = f32[32,2048]{0,1:T(8,128)} async-done(((f32[32,2048]{0,1:T(8,128)}), f32[32,2048]{0,1:T(8,128)}) %all-reduce.4.cloned.1.call-update) | async-done | bytes 262160 | tf_op jit(solution)/shard_map/psum | solution.py:51
  717.9 2.2 copy.138
  720.2 0.0 all-gather.2.cloned.1.call-update
  720.2 0.0 all-reduce.6.cloned.1.call-start
  720.3 0.0 copy-done.3
  720.3 0.6 dynamic-slice.1
  721.5 0.0 copy-done
  721.5 8.9 convolution_bitcast_fusion.1
  730.4 104.7 %psum.22 = f32[32]{0:T(128)S(1)} all-reduce(f32[32]{0:T(128)S(1)} %convolution_bitcast_fusion.1), channel_id=1, replica_groups=mesh['row'=64,'col'=4] {'row'}, use_global_device_ids=true, to_apply=%region_3.4 | all-reduce | flops 32 | bytes 256 | tf_op jit(solution)/shard_map/psum | solution.py:51
  835.1 0.2 dynamic-update-slice.3
  835.3 10.7 %all-reduce = f32[128]{0:T(128)S(1)} all-reduce(f32[128]{0:T(128)S(1)} %dynamic-update-slice.3), channel_id=1, replica_groups=mesh['row'=64,'col'=4] {'col'}, use_global_device_ids=true, to_apply=%add | all-reduce | flops 128 | bytes 1024
  846.1 2.6 fusion.94
  848.6 0.1 copy.139
  848.7 11.7 %cholesky.16 = f32[128,128]{1,0:T(8,128)S(1)} custom-call(f32[128,128]{1,0:T(8,128)S(1)} %fusion.34), custom_call_target="Cholesky" | custom-call | tf_op jit(solution)/shard_map/jit(cholesky)/cholesky | solution.py:57
  860.5 0.6 compare_reduce_fusion
  861.1 0.7 fusion.23
  861.8 9.8 %custom-call.8 = f32[1,128,128]{1,2,0:T(8,128)S(1)} custom-call(f32[1,128,128]{2,1,0:T(8,128)S(1)} %fusion.23), custom_call_target="InvertDiagBlocksLowerTriangular" | custom-call | tf_op jit(solution)/shard_map/triangular_solve | solution.py:58
  871.6 0.2 fusion.32
  871.8 0.2 convolution_bitcast_fusion.2
  872.0 7.1 fusion.63
  879.0 0.0 all-reduce.6.cloned.1.call-update
  879.0 59.2 %all-reduce.6.cloned.1.call-done = f32[65536]{0:T(1024)} async-done(((f32[65536]{0:T(1024)}), f32[65536]{0:T(1024)}) %all-reduce.6.cloned.1.call-update) | async-done | bytes 262160 | tf_op jit(solution)/shard_map/psum | solution.py:67
  938.3 1.7 sub.22
  940.0 0.0 copy-done.2
  (72 shorter events, 1.9 us)
Async XLA Ops:
  302.2 8.1 copy-start.1
  302.2 192.3 %all-to-all-start.1 = ((f32[32,64,1024]{2,0,1:T(8,128)}), f32[32,64,1024]{2,0,1:T(8,128)}, u32[]{:S(2)}, u32[]{:S(2)}) async-start(f32[32,64,1024]{2,0,1:T(8,128)} %copy.136), calls=%async_computation.1 | async-start | bytes 16777216 | tf_op jit(solution)/shard_map/all_to_all | solution.py:41
  310.2 407.7 %all-reduce.4.cloned.1.call-start = ((), (), s32[]{:S(2)}) async-start(), calls=%async_computation.2 | async-start | bytes 2097152 | tf_op jit(solution)/shard_map/psum | solution.py:51
  310.4 409.9 %copy-start.3 = (u32[256]{0:T(256)S(1)}, u32[256]{0:T(256)}, u32[]{:S(2)}) copy-start(u32[256]{0:T(256)} %constant.164) | copy-start | bytes 3076
  310.4 411.1 %copy-start = (f32[65536]{0:T(1024)S(1)}, f32[65536]{0:T(1024)}, u32[]{:S(2)}) copy-start(f32[65536]{0:T(1024)} %param.7) | copy-start | bytes 786436
  532.5 313.6 %all-gather.2.cloned.1.call-start = ((), (), s32[]{:S(2)}) async-start(), calls=%async_computation.3 | async-start | bytes 1310720 | tf_op jit(solution)/shard_map/all_gather | solution.py:53
  720.2 218.1 %all-reduce.6.cloned.1.call-start = ((), (), s32[]{:S(2)}) async-start(), calls=%async_computation.4 | async-start | bytes 524288 | tf_op jit(solution)/shard_map/psum | solution.py:67
  871.8 68.2 %copy-start.2 = (f32[1,128]{1,0:T(1,128)}, f32[1,128]{1,0:T(1,128)S(1)}, u32[]{:S(2)}) copy-start(f32[1,128]{1,0:T(1,128)S(1)} %fusion.32) | copy-start | bytes 1540
Sparse Core Ops, SparseCore 0:
  532.6 185.2 all-reduce.3
  720.3 23.8 all-gather.1
  879.2 59.0 all-reduce.5
